TPU v7x, 512 devices: a whole 4x4x16 slice. The times are simulated.
512 devices in a mesh: dp: 32 (over z, core), cent: 16 (over x, y).
Axes of the slice: x: 4, y: 4, z: 16, core: 2. Of those that a mesh axis runs over, the one named last changes fastest.
Arguments:
- embeddings: bfloat16 [262144, 1024], P(('dp', 'cent')), may hold values from -44.5 to 53.875
- centroids: float32 [131072, 1024], P(('dp', 'cent')), may hold values from -3 to 5
- candidates: int32 [1024, 8], P(('dp', 'cent')), may hold values from 0 to 15, all different within a row; in each aligned block of 32 rows (0 to 31, 32 to 63, ...) at most 24 rows name the same one
Outputs:
- new_centroids: float32 [131072, 1024], P(('dp', 'cent'))
- log_norm: float32 [262144], P(('dp', 'cent'))
- objective: float32 [], replicated
Inputs may be any that keep to these rules, and one draw needn't show every extreme that they name: `candidates`: the 8 entries of a row block are different. Among the row blocks of one coarse group (aligned runs of 32 row blocks), no centroid block is named more than 24 times, and some centroid block is named exactly 24 times in every draw.
All inputs are finite; a program needn't handle non-finite values.
Results may differ from a plain program's by a relative error of at most 0.0067.
Values may be sent and summed in bfloat16 or wider, within the bound.
No kernel may reach another device: no remote copies, remote signals or barrier semaphores. Data moves between devices by JAX's collectives and lax.ppermute only.
A program may use at most 128 MiB of HBM per device.

v0:
```python
import math
import jax
import jax.numpy as jnp
from jax import lax
from jax.sharding import PartitionSpec as P

BLK = 256
TOPC = 8
floor_value = -1e30


def per_device(embeddings, centroids, candidates):
    cent_count = lax.axis_size("cent")
    own_index = lax.axis_index("cent")
    block_len = BLK
    feature_dim = embeddings.shape[1]
    own_row_blocks = candidates.shape[0]
    own_blocks = centroids.shape[0] // block_len
    group_blocks = own_row_blocks * cent_count
    slot_count = min(own_row_blocks * cent_count, 3 * own_row_blocks * TOPC // (2 * own_blocks))
    cent_blocks = centroids.astype(jnp.bfloat16).reshape(own_blocks, block_len, feature_dim)
    half_norm = 0.5 * jnp.sum(centroids * centroids, axis=1).reshape(own_blocks, block_len)
    group_rows, group_lists = (
        lax.all_gather(embeddings, "cent", axis=0, tiled=True),
        lax.all_gather(candidates, "cent", axis=0, tiled=True),
    )
    grouped = group_rows.reshape(group_blocks, block_len, feature_dim)
    own_ids = own_index * own_blocks + jnp.arange(own_blocks, dtype=jnp.int32)
    requested = jnp.any(group_lists[:, :, None] == own_ids[None, None, :], axis=1)
    block_iota = jnp.arange(group_blocks, dtype=jnp.int32)
    sort_keys = jnp.where(requested, 0, group_blocks) + block_iota[:, None]
    slot_blocks = jnp.argsort(sort_keys, axis=0)[:slot_count]
    slot_live = jnp.take_along_axis(requested, slot_blocks, axis=0)
    picked = grouped[slot_blocks]
    dot_scores = jnp.einsum(
        "mjbd,jkd->mjbk", picked, cent_blocks, preferred_element_type=jnp.float32
    )
    live_mask = slot_live[:, :, None, None]
    logits = (dot_scores - half_norm[None, :, None, :]) / math.sqrt(feature_dim)
    logits = jnp.where(live_mask, logits, floor_value)
    local_peak = jnp.max(logits, axis=3)
    local_total = jnp.where(
        slot_live[:, :, None], jnp.sum(jnp.exp(logits - local_peak[..., None]), axis=3), 0.0
    )
    peak_rows = (
        jnp.full((group_blocks, block_len), floor_value, jnp.float32)
        .at[slot_blocks]
        .max(local_peak)
    )
    scaled_total = local_total * jnp.exp(local_peak - peak_rows[slot_blocks])
    total_rows = jnp.zeros((group_blocks, block_len), jnp.float32).at[slot_blocks].add(scaled_total)
    global_peak = lax.pmax(peak_rows.astype(jnp.bfloat16), "cent").astype(peak_rows.dtype)
    global_total = lax.psum(total_rows * jnp.exp(peak_rows - global_peak), "cent")
    log_group = global_peak + jnp.log(global_total)
    log_norm = lax.dynamic_slice_in_dim(
        log_group, own_index * own_row_blocks, own_row_blocks, 0
    ).reshape(-1)
    weights = jnp.where(live_mask, jnp.exp(logits - log_group[slot_blocks][..., None]), 0.0)
    counts = jnp.sum(weights, axis=(0, 2))
    weights_bf = weights.astype(jnp.bfloat16)
    block_sums = jnp.einsum(
        "mjbk,mjbd->jkd", weights_bf, picked, preferred_element_type=jnp.float32
    )
    old_blocks = centroids.reshape(own_blocks, block_len, feature_dim)
    new_blocks = (block_sums + old_blocks) / (counts[..., None] + 1.0)
    new_centroids = new_blocks.reshape(own_blocks * block_len, feature_dim)
    row_total_count = embeddings.shape[0] * lax.axis_size("dp") * cent_count
    objective = lax.psum(jnp.sum(log_norm), ("dp", "cent")) / row_total_count
    return (new_centroids, log_norm, objective)


def solution(mesh):
    in_specs = (P(("dp", "cent"), None), P(("dp", "cent"), None), P(("dp", "cent"), None))
    out_specs = (P(("dp", "cent"), None), P(("dp", "cent")), P())
    return jax.shard_map(
        per_device, mesh=mesh, in_specs=in_specs, out_specs=out_specs, check_vma=False
    )
```

profile of v0, /device:TPU:1, one launch (start us, length us, event | category | flops | bytes accessed | tf_op | source)
XLA Modules:
  0.0 435.2 jit_solution(5110639029860988073)
XLA Ops:
  7.2 0.0 all-gather.3.cloned.1.call-start
  7.2 0.7 all-gather.3.cloned.1.call-update
  7.9 19.6 %all-gather = s32[16,2,8]{2,1,0:T(2,128)S(1)} all-gather(s32[1,2,8]{2,1,0:T(2,128)} %bitcast.88), channel_id=1, replica_groups=mesh['dp'=32,'cent'=16] {'cent'}, dimensions={0}, use_global_device_ids=true | all-gather | bytes 1088 | tf_op jit(solution)/shard_map/all_gather | solution.py:25
  27.5 0.4 compare_reduce_fusion
  27.8 0.1 reshape.211
  28.0 0.1 copy.10
  28.1 0.8 sort.17
  28.9 0.1 fusion.37
  29.0 0.7 gather_fusion
  29.7 0.1 copy.11
  29.8 0.1 select_reduce_fusion
  29.9 1.4 multiply_reduce_fusion
  31.3 111.3 %all-gather.3.cloned.1.call-done = bf16[8192,1024]{1,0:T(8,128)(2,1)} async-done(((bf16[512,1024]{1,0:T(8,128)(2,1)}), bf16[8192,1024]{1,0:T(8,128)(2,1)}) %all-gather.3.cloned.1.call-update) | async-done | bytes 16777232 | tf_op jit(solution)/shard_map/all_gather | solution.py:24
  142.6 0.0 copy-start.2
  142.7 12.0 %gather_fusion.1 = bf16[24,256,1024]{2,1,0:T(8,128)(2,1)} fusion(bf16[32,256,1024]{2,1,0:T(8,128)(2,1)} %bitcast.85, s32[1024]{0:T(1024)S(1)} %pad_clamp_fusion), kind=kCustom, calls=%fused_computation.1 | custom fusion | bytes 25165920 | tf_op jit(solution)/shard_map/gather | solution.py:34
  154.6 0.0 copy-done.2
  154.6 6.6 %fusion.11 = (f32[24,256]{1,0:T(8,128)S(1)}, f32[24,256,256]{1,2,0:T(8,128)S(1)}) fusion(f32[256]{0:T(256)S(1)} %broadcast_multiply_fusion, pred[24]{0:T(512)(128)(4,1)S(1)} %select_reduce_fusion, bf16[24,256,1024]{2,1,0:T(8,128)(2,1)} %gather_fusion.1, f32[256,1024]{1,0:T(8,128)S(1)} %copy-done.2), kind=kOutput, calls=%fused_computation.18 | convolution fusion | flops 3227772928 | bytes 19948568 | tf_op jit(solution)/shard_map/mjbd,jkd->mjbk/dot_general | solution.py:35
  161.3 0.0 copy-start
  161.3 2.7 copy-done
  163.9 1.8 exponential_reduce_fusion
  165.8 0.7 scatter_custom_fusion
  166.5 58.2 %pmax.7 = bf16[32,256]{1,0:T(8,128)(2,1)S(1)} all-reduce(bf16[32,256]{1,0:T(8,128)(2,1)S(1)} %convert_element_type.13), channel_id=1, replica_groups=mesh['dp'=32,'cent'=16] {'cent'}, use_global_device_ids=true, to_apply=%region_5.6 | all-reduce | flops 8192 | bytes 32768 | tf_op jit(solution)/shard_map/pmax | solution.py:52
  224.7 0.8 scatter_custom_fusion.1
  225.6 55.6 %psum.14 = f32[32,256]{1,0:T(8,128)S(1)} all-reduce(f32[32,256]{1,0:T(8,128)S(1)} %fusion.27), channel_id=1, replica_groups=mesh['dp'=32,'cent'=16] {'cent'}, use_global_device_ids=true, to_apply=%region_8.9 | all-reduce | flops 8192 | bytes 65536 | tf_op jit(solution)/shard_map/psum | solution.py:53
  281.2 0.6 gather_fusion.2
  281.8 0.0 copy-start.1
  281.8 4.5 %fusion.3 = f32[256]{0:T(256)S(1)} fusion(f32[24,256]{1,0:T(8,128)S(1)} %gather_fusion.2, f32[256]{0:T(256)S(1)} %broadcast_multiply_fusion, f32[24,256,256]{1,2,0:T(8,128)} %copy-done, pred[24]{0:T(512)(128)(4,1)S(1)} %select_reduce_fusion), kind=kLoop, calls=%fused_computation.12 | loop fusion | flops 9436928 | bytes 6318104 | tf_op jit(solution)/shard_map/reduce_sum | solution.py:59
  286.3 0.1 copy-done.1
  286.4 9.3 %fusion.20 = f32[256,1024]{1,0:T(8,128)} fusion(f32[256,1024]{1,0:T(8,128)S(1)} %copy-done.2, bf16[24,256,1024]{2,1,0:T(8,128)(2,1)} %gather_fusion.1, f32[24,256]{1,0:T(8,128)S(1)} %gather_fusion.2, f32[256]{0:T(256)S(1)} %broadcast_multiply_fusion, f32[24,256,256]{1,2,0:T(8,128)S(1)} %copy-done.1, pred[24]{0:T(512)(128)(4,1)S(1)} %select_reduce_fusion, ...), kind=kOutput, calls=%fused_computation.23 | convolution fusion | flops 3231186944 | bytes 20998168 | tf_op jit(solution)/shard_map/mjbk,mjbd->jkd/dot_general | solution.py:61
  295.8 0.6 dynamic-slice_reduce_fusion
  296.4 0.6 copy.12
  296.9 129.6 %psum.15 = f32[]{:T(128)} all-reduce(f32[]{:T(128)} %get-tuple-element.5), channel_id=1, replica_groups=mesh['dp'=32,'cent'=16] {'dp','cent'}, use_global_device_ids=true, to_apply=%region_11.12 | all-reduce | flops 1 | bytes 8 | tf_op jit(solution)/shard_map/psum | solution.py:68
  (9 shorter events, 0.1 us)
Async XLA Ops:
  7.2 135.5 %all-gather.3.cloned.1.call-start = ((), (), s32[]{:S(2)}) async-start(), calls=%async_computation | async-start | bytes 17825792 | tf_op jit(solution)/shard_map/all_gather | solution.py:24
  142.6 12.0 %copy-start.2 = (f32[256,1024]{1,0:T(8,128)S(1)}, f32[256,1024]{1,0:T(8,128)}, u32[]{:S(2)}) copy-start(f32[256,1024]{1,0:T(8,128)} %param.4) | copy-start | bytes 3145732
  161.3 2.7 copy-start
  281.8 4.6 %copy-start.1 = (f32[24,256,256]{1,2,0:T(8,128)S(1)}, f32[24,256,256]{1,2,0:T(8,128)}, u32[]{:S(2)}) copy-start(f32[24,256,256]{1,2,0:T(8,128)} %copy-done) | copy-start | bytes 18874372
Sparse Core Ops, SparseCore 0:
  11.0 131.6 all-gather.2
where the time goes:
time: 436 us; the launch traced here: 435 us
  blocking collectives  263 us (60%)
  waiting for transfers between devices  112 us (26%)
  local copies, waits for them, and re-layouts  16.9 us (4%)
  matrix products  15.9 us (4%)
  between operations  15.9 us (4%)
  other arithmetic  11.3 us (3%)
    psum x1, blocking collectives, per_device(): objective = lax.psum(jnp.sum(log_norm), ('dp', 'cent')) / row_total_count  130 us
    all_gather x1, waiting for transfers between devices, per_device(): lax.all_gather(embeddings, 'cent', axis=0, tiled=True)  111 us
    pmax x1, blocking collectives, per_device(): lax.pmax(peak_rows.astype(jnp.bfloat16), 'cent').astype(peak_rows.dtype)  58.2 us
    psum x1, blocking collectives, per_device(): lax.psum(total_rows * jnp.exp(peak_rows - global_peak), 'cent')  55.6 us
    all_gather x1, blocking collectives, per_device(): lax.all_gather(candidates, 'cent', axis=0, tiled=True)  19.6 us
    gather x1, local copies, waits for them, and re-layouts, per_device(): picked = grouped[slot_blocks]  12 us
    dot_general x1, matrix products, per_device(): jnp.einsum('mjbk,mjbd->jkd', weights_bf, picked, preferred_element_type=j...  9.32 us
  transfers between devices with their start and end apart: 1, of which 1 were waited for; matrix products, arithmetic and copies ran while one was open for 1% of the time, Pallas kernels for 0%

commit v1 on v0

--- a/solution.py
+++ b/solution.py
@@ -7,6 +7,13 @@
 BLK = 256
 TOPC = 8
 floor_value = -1e30
+
+
+def gather_over(x, axis, dim):
+    peers = lax.axis_size(axis)
+    blocks = jnp.stack([x for _ in range(peers)])
+    blocks = lax.all_to_all(blocks, axis, split_axis=0, concat_axis=0)
+    return jnp.concatenate(blocks, axis=dim)
 
 
 def per_device(embeddings, centroids, candidates):
@@ -22,7 +29,7 @@
     half_norm = 0.5 * jnp.sum(centroids * centroids, axis=1).reshape(own_blocks, block_len)
     group_rows, group_lists = (
         lax.all_gather(embeddings, "cent", axis=0, tiled=True),
-        lax.all_gather(candidates, "cent", axis=0, tiled=True),
+        gather_over(candidates, "cent", 0),
     )
     grouped = group_rows.reshape(group_blocks, block_len, feature_dim)
     own_ids = own_index * own_blocks + jnp.arange(own_blocks, dtype=jnp.int32)

time: 436 us -> 436 us (level)
  blocking collectives: 263 us -> 243 us
  waiting for transfers between devices: 112 us -> 123 us
  starting transfers between devices: 0.04 us -> 7.61 us
    all_gather x1 -> x0, blocking collectives: 19.6 us -> none  [per_device(): lax.all_gather(candidates, 'cent', axis=0, tiled=True)]
    all_to_all x0 -> x1, starting transfers between devices: none -> 7.57 us  [gather_over(): blocks = lax.all_to_all(blocks, axis, split_axis=0, concat_axis=0)]
    all_gather x1, waiting for transfers between devices: 111 us -> 117 us  [per_device(): lax.all_gather(embeddings, 'cent', axis=0, tiled=True)]
    all_to_all x0 -> x1, waiting for transfers between devices: none -> 5.07 us  [gather_over(): blocks = lax.all_to_all(blocks, axis, split_axis=0, concat_axis=0)]
  transfers between devices with their start and end apart: 1 -> 2, of which waited for: 1 -> 2; matrix products, arithmetic and copies ran while one was open for 1% -> 1% of each run, Pallas kernels for 0% -> 0%
where the time goes in v1:
time: 436 us; the launch traced here: 435 us
  blocking collectives  243 us (56%)
  waiting for transfers between devices  123 us (28%)
  local copies, waits for them, and re-layouts  18.4 us (4%)
  matrix products  15.9 us (4%)
  between operations  15.9 us (4%)
  other arithmetic  11 us (3%)
  starting transfers between devices  7.61 us (2%)
    psum x1, blocking collectives, per_device(): objective = lax.psum(jnp.sum(log_norm), ('dp', 'cent')) / row_total_count  130 us
    all_gather x1, waiting for transfers between devices, per_device(): lax.all_gather(embeddings, 'cent', axis=0, tiled=True)  117 us
    pmax x1, blocking collectives, per_device(): lax.pmax(peak_rows.astype(jnp.bfloat16), 'cent').astype(peak_rows.dtype)  58.2 us
    psum x1, blocking collectives, per_device(): lax.psum(total_rows * jnp.exp(peak_rows - global_peak), 'cent')  55.6 us
    gather x1, local copies, waits for them, and re-layouts, per_device(): picked = grouped[slot_blocks]  12 us
    dot_general x1, matrix products, per_device(): jnp.einsum('mjbk,mjbd->jkd', weights_bf, picked, preferred_element_type=j...  9.3 us
  transfers between devices with their start and end apart: 2, of which 2 were waited for; matrix products, arithmetic and copies ran while one was open for 1% of the time, Pallas kernels for 0%

profile of v1, /device:TPU:1, one launch (start us, length us, event | category | flops | bytes accessed | tf_op | source)
XLA Modules:
  0.0 435.2 jit_solution(3675581800869291137)
XLA Ops:
  7.2 0.0 all-gather.2.cloned.1.call-start
  7.2 0.7 all-gather.2.cloned.1.call-update
  7.9 1.3 stack.2
  9.2 7.6 %all-to-all-start = ((s32[16,2,8]{2,1,0:T(2,128)}), s32[16,2,8]{2,1,0:T(2,128)S(1)}, u32[]{:S(2)}, u32[]{:S(2)}) async-start(s32[16,2,8]{2,1,0:T(2,128)} %stack.2), calls=%async_computation | async-start | bytes 32768 | tf_op jit(solution)/shard_map/all_to_all | solution.py:15
  16.8 1.4 multiply_reduce_fusion
  18.2 5.1 %all-to-all-done = s32[16,2,8]{2,1,0:T(2,128)S(1)} async-done(((s32[16,2,8]{2,1,0:T(2,128)}), s32[16,2,8]{2,1,0:T(2,128)S(1)}, u32[]{:S(2)}, u32[]{:S(2)}) %all-to-all-start) | async-done | bytes 1056 | tf_op jit(solution)/shard_map/all_to_all | solution.py:15
  23.2 0.1 copy.19
  23.3 0.1 copy.22
  23.4 0.1 copy.20
  23.5 0.1 reshape.216
  23.6 0.1 reshape.150
  23.7 0.8 sort.17
  24.5 0.1 fusion.37
  24.6 0.7 gather_fusion
  25.3 0.1 copy.23
  25.4 0.1 select_reduce_fusion
  25.6 117.1 %all-gather.2.cloned.1.call-done = bf16[8192,1024]{1,0:T(8,128)(2,1)} async-done(((bf16[512,1024]{1,0:T(8,128)(2,1)}), bf16[8192,1024]{1,0:T(8,128)(2,1)}) %all-gather.2.cloned.1.call-update) | async-done | bytes 16777232 | tf_op jit(solution)/shard_map/all_gather | solution.py:31
  142.7 12.0 %gather_fusion.1 = bf16[24,256,1024]{2,1,0:T(8,128)(2,1)} fusion(bf16[32,256,1024]{2,1,0:T(8,128)(2,1)} %bitcast.82, s32[1024]{0:T(1024)S(1)} %pad_clamp_fusion), kind=kCustom, calls=%fused_computation.1 | custom fusion | bytes 25165920 | tf_op jit(solution)/shard_map/gather | solution.py:41
  154.6 6.6 %fusion.11 = (f32[24,256]{1,0:T(8,128)S(1)}, f32[24,256,256]{1,2,0:T(8,128)S(1)}) fusion(f32[256]{0:T(256)S(1)} %broadcast_multiply_fusion, pred[24]{0:T(512)(128)(4,1)S(1)} %select_reduce_fusion, bf16[24,256,1024]{2,1,0:T(8,128)(2,1)} %gather_fusion.1, f32[256,1024]{1,0:T(8,128)S(1)} %copy-done.2), kind=kOutput, calls=%fused_computation.18 | convolution fusion | flops 3227772928 | bytes 19948568 | tf_op jit(solution)/shard_map/mjbd,jkd->mjbk/dot_general | solution.py:42
  161.3 2.7 copy-done
  163.9 1.8 exponential_reduce_fusion
  165.8 0.7 scatter_custom_fusion
  166.5 58.2 %pmax.7 = bf16[32,256]{1,0:T(8,128)(2,1)S(1)} all-reduce(bf16[32,256]{1,0:T(8,128)(2,1)S(1)} %convert_element_type.13), channel_id=1, replica_groups=mesh['dp'=32,'cent'=16] {'cent'}, use_global_device_ids=true, to_apply=%region_5.6 | all-reduce | flops 8192 | bytes 32768 | tf_op jit(solution)/shard_map/pmax | solution.py:59
  224.8 0.8 scatter_custom_fusion.1
  225.6 55.6 %psum.14 = f32[32,256]{1,0:T(8,128)S(1)} all-reduce(f32[32,256]{1,0:T(8,128)S(1)} %fusion.27), channel_id=1, replica_groups=mesh['dp'=32,'cent'=16] {'cent'}, use_global_device_ids=true, to_apply=%region_8.9 | all-reduce | flops 8192 | bytes 65536 | tf_op jit(solution)/shard_map/psum | solution.py:60
  281.2 0.6 gather_fusion.2
  281.8 4.5 %fusion.3 = f32[256]{0:T(256)S(1)} fusion(f32[24,256]{1,0:T(8,128)S(1)} %gather_fusion.2, f32[256]{0:T(256)S(1)} %broadcast_multiply_fusion, f32[24,256,256]{1,2,0:T(8,128)} %copy-done, pred[24]{0:T(512)(128)(4,1)S(1)} %select_reduce_fusion), kind=kLoop, calls=%fused_computation.12 | loop fusion | flops 9436928 | bytes 6318104 | tf_op jit(solution)/shard_map/reduce_sum | solution.py:66
  286.4 0.1 copy-done.1
  286.5 9.3 %fusion.20 = f32[256,1024]{1,0:T(8,128)} fusion(f32[256,1024]{1,0:T(8,128)S(1)} %copy-done.2, bf16[24,256,1024]{2,1,0:T(8,128)(2,1)} %gather_fusion.1, f32[24,256]{1,0:T(8,128)S(1)} %gather_fusion.2, f32[256]{0:T(256)S(1)} %broadcast_multiply_fusion, f32[24,256,256]{1,2,0:T(8,128)S(1)} %copy-done.1, pred[24]{0:T(512)(128)(4,1)S(1)} %select_reduce_fusion, ...), kind=kOutput, calls=%fused_computation.23 | convolution fusion | flops 3231186944 | bytes 20998168 | tf_op jit(solution)/shard_map/mjbk,mjbd->jkd/dot_general | solution.py:68
  295.8 0.6 dynamic-slice_reduce_fusion
  296.4 0.6 copy.24
  296.9 129.6 %psum.15 = f32[]{:T(128)} all-reduce(f32[]{:T(128)} %get-tuple-element.5), channel_id=1, replica_groups=mesh['dp'=32,'cent'=16] {'dp','cent'}, use_global_device_ids=true, to_apply=%region_11.12 | all-reduce | flops 1 | bytes 8 | tf_op jit(solution)/shard_map/psum | solution.py:75
  (14 shorter events, 0.1 us)
Async XLA Ops:
  7.2 135.5 %all-gather.2.cloned.1.call-start = ((), (), s32[]{:S(2)}) async-start(), calls=%async_computation.1 | async-start | bytes 17825792 | tf_op jit(solution)/shard_map/all_gather | solution.py:31
  9.2 14.0 %all-to-all-start = ((s32[16,2,8]{2,1,0:T(2,128)}), s32[16,2,8]{2,1,0:T(2,128)S(1)}, u32[]{:S(2)}, u32[]{:S(2)}) async-start(s32[16,2,8]{2,1,0:T(2,128)} %stack.2), calls=%async_computation | async-start | bytes 32768 | tf_op jit(solution)/shard_map/all_to_all | solution.py:15
  142.7 12.0 %copy-start.2 = (f32[256,1024]{1,0:T(8,128)S(1)}, f32[256,1024]{1,0:T(8,128)}, u32[]{:S(2)}) copy-start(f32[256,1024]{1,0:T(8,128)} %param.4) | copy-start | bytes 3145732
  161.3 2.7 copy-start
  281.8 4.6 %copy-start.1 = (f32[24,256,256]{1,2,0:T(8,128)S(1)}, f32[24,256,256]{1,2,0:T(8,128)}, u32[]{:S(2)}) copy-start(f32[24,256,256]{1,2,0:T(8,128)} %copy-done) | copy-start | bytes 18874372
Sparse Core Ops, SparseCore 0:
  11.0 131.6 all-gather.1

commit v2 on v0

--- a/solution.py
+++ b/solution.py
@@ -7,6 +7,12 @@
 BLK = 256
 TOPC = 8
 floor_value = -1e30
+
+
+def gather_and_add(block, axis):
+    parts = lax.all_gather(block, axis, axis=0, tiled=False)
+    result = parts.sum(axis=0)
+    return result
 
 
 def per_device(embeddings, centroids, candidates):
@@ -50,7 +56,7 @@
     scaled_total = local_total * jnp.exp(local_peak - peak_rows[slot_blocks])
     total_rows = jnp.zeros((group_blocks, block_len), jnp.float32).at[slot_blocks].add(scaled_total)
     global_peak = lax.pmax(peak_rows.astype(jnp.bfloat16), "cent").astype(peak_rows.dtype)
-    global_total = lax.psum(total_rows * jnp.exp(peak_rows - global_peak), "cent")
+    global_total = gather_and_add(total_rows * jnp.exp(peak_rows - global_peak), "cent")
     log_group = global_peak + jnp.log(global_total)
     log_norm = lax.dynamic_slice_in_dim(
         log_group, own_index * own_row_blocks, own_row_blocks, 0

time: 436 us -> 390 us (0.89)
  blocking collectives: 263 us -> 217 us
    psum x1 -> x0, blocking collectives: 55.6 us -> none  [per_device(): lax.psum(total_rows * jnp.exp(peak_rows - global_peak), 'cent')]
    all_gather x0 -> x1, blocking collectives: none -> 16 us  [gather_and_add(): parts = lax.all_gather(block, axis, axis=0, tiled=False)]
    psum x1, blocking collectives: 130 us -> 124 us  [per_device(): objective = lax.psum(jnp.sum(log_norm), ('dp', 'cent')) / row_total_count]
where the time goes in v2:
time: 390 us
  blocking collectives  217 us (56%)
  waiting for transfers between devices  112 us (29%)
  local copies, waits for them, and re-layouts  16.9 us (4%)
  matrix products  15.9 us (4%)
  between operations  15.9 us (4%)
  other arithmetic  11.4 us (3%)
    psum x1, blocking collectives, per_device(): objective = lax.psum(jnp.sum(log_norm), ('dp', 'cent')) / row_total_count  124 us
    all_gather x1, waiting for transfers between devices, per_device(): lax.all_gather(embeddings, 'cent', axis=0, tiled=True)  111 us
    pmax x1, blocking collectives, per_device(): lax.pmax(peak_rows.astype(jnp.bfloat16), 'cent').astype(peak_rows.dtype)  58.2 us
    all_gather x1, blocking collectives, per_device(): lax.all_gather(candidates, 'cent', axis=0, tiled=True)  19.6 us
    all_gather x1, blocking collectives, gather_and_add(): parts = lax.all_gather(block, axis, axis=0, tiled=False)  16 us
    gather x1, local copies, waits for them, and re-layouts, per_device(): picked = grouped[slot_blocks]  12 us
    dot_general x1, matrix products, per_device(): jnp.einsum('mjbk,mjbd->jkd', weights_bf, picked, preferred_element_type=j...  9.32 us
  transfers between devices with their start and end apart: 1, of which 1 were waited for; matrix products, arithmetic and copies ran while one was open for 1% of the time, Pallas kernels for 0%

profile of v2, /device:TPU:1, one launch (start us, length us, event | category | flops | bytes accessed | tf_op | source)
XLA Modules:
  0.0 389.5 jit_solution(532749366786340140)
XLA Ops:
  7.2 0.0 all-gather.4.cloned.1.call-start
  7.2 0.7 all-gather.4.cloned.1.call-update
  7.9 19.6 %all-gather.1 = s32[16,2,8]{2,1,0:T(2,128)S(1)} all-gather(s32[1,2,8]{2,1,0:T(2,128)} %bitcast.90), channel_id=1, replica_groups=mesh['dp'=32,'cent'=16] {'cent'}, dimensions={0}, use_global_device_ids=true | all-gather | bytes 1088 | tf_op jit(solution)/shard_map/all_gather | solution.py:31
  27.5 0.4 compare_reduce_fusion
  27.8 0.1 reshape.212
  28.0 0.1 copy.10
  28.1 0.8 sort.17
  28.9 0.1 fusion.37
  29.0 0.7 gather_fusion
  29.7 0.1 copy.11
  29.8 0.1 select_reduce_fusion
  29.9 1.4 multiply_reduce_fusion
  31.3 111.3 %all-gather.4.cloned.1.call-done = bf16[8192,1024]{1,0:T(8,128)(2,1)} async-done(((bf16[512,1024]{1,0:T(8,128)(2,1)}), bf16[8192,1024]{1,0:T(8,128)(2,1)}) %all-gather.4.cloned.1.call-update) | async-done | bytes 16777232 | tf_op jit(solution)/shard_map/all_gather | solution.py:30
  142.6 0.0 copy-start.2
  142.7 12.0 %gather_fusion.1 = bf16[24,256,1024]{2,1,0:T(8,128)(2,1)} fusion(bf16[32,256,1024]{2,1,0:T(8,128)(2,1)} %bitcast.86, s32[1024]{0:T(1024)S(1)} %pad_clamp_fusion), kind=kCustom, calls=%fused_computation.1 | custom fusion | bytes 25165920 | tf_op jit(solution)/shard_map/gather | solution.py:40
  154.6 0.0 copy-done.2
  154.6 6.6 %fusion.11 = (f32[24,256]{1,0:T(8,128)S(1)}, f32[24,256,256]{1,2,0:T(8,128)S(1)}) fusion(f32[256]{0:T(256)S(1)} %broadcast_multiply_fusion, pred[24]{0:T(512)(128)(4,1)S(1)} %select_reduce_fusion, bf16[24,256,1024]{2,1,0:T(8,128)(2,1)} %gather_fusion.1, f32[256,1024]{1,0:T(8,128)S(1)} %copy-done.2), kind=kOutput, calls=%fused_computation.18 | convolution fusion | flops 3227772928 | bytes 19948568 | tf_op jit(solution)/shard_map/mjbd,jkd->mjbk/dot_general | solution.py:41
  161.3 0.0 copy-start
  161.3 2.7 copy-done
  163.9 1.8 exponential_reduce_fusion
  165.8 0.7 scatter_custom_fusion
  166.5 58.2 %pmax.7 = bf16[32,256]{1,0:T(8,128)(2,1)S(1)} all-reduce(bf16[32,256]{1,0:T(8,128)(2,1)S(1)} %convert_element_type.13), channel_id=1, replica_groups=mesh['dp'=32,'cent'=16] {'cent'}, use_global_device_ids=true, to_apply=%region_5.6 | all-reduce | flops 8192 | bytes 32768 | tf_op jit(solution)/shard_map/pmax | solution.py:58
  224.7 0.8 scatter_custom_fusion.1
  225.6 16.0 %all-gather = f32[512,256]{1,0:T(8,128)S(1)} all-gather(f32[32,256]{1,0:T(8,128)S(1)} %fusion.27), channel_id=2, replica_groups=mesh['dp'=32,'cent'=16] {'cent'}, dimensions={0}, use_global_device_ids=true | all-gather | bytes 557056 | tf_op jit(solution)/shard_map/all_gather | solution.py:13
  241.6 0.6 gather_fusion.2
  242.2 0.0 copy-start.1
  242.2 4.5 %fusion.3 = f32[256]{0:T(256)S(1)} fusion(f32[24,256]{1,0:T(8,128)S(1)} %gather_fusion.2, f32[256]{0:T(256)S(1)} %broadcast_multiply_fusion, f32[24,256,256]{1,2,0:T(8,128)} %copy-done, pred[24]{0:T(512)(128)(4,1)S(1)} %select_reduce_fusion), kind=kLoop, calls=%fused_computation.12 | loop fusion | flops 9436928 | bytes 6318104 | tf_op jit(solution)/shard_map/reduce_sum | solution.py:65
  246.8 0.1 copy-done.1
  246.9 9.3 %fusion.20 = f32[256,1024]{1,0:T(8,128)} fusion(f32[256,1024]{1,0:T(8,128)S(1)} %copy-done.2, bf16[24,256,1024]{2,1,0:T(8,128)(2,1)} %gather_fusion.1, f32[24,256]{1,0:T(8,128)S(1)} %gather_fusion.2, f32[256]{0:T(256)S(1)} %broadcast_multiply_fusion, f32[24,256,256]{1,2,0:T(8,128)S(1)} %copy-done.1, pred[24]{0:T(512)(128)(4,1)S(1)} %select_reduce_fusion, ...), kind=kOutput, calls=%fused_computation.23 | convolution fusion | flops 3231186944 | bytes 20998168 | tf_op jit(solution)/shard_map/mjbk,mjbd->jkd/dot_general | solution.py:67
  256.2 0.6 dynamic-slice_reduce_fusion
  256.8 0.6 copy.12
  257.4 123.5 %psum.7 = f32[]{:T(128)} all-reduce(f32[]{:T(128)} %get-tuple-element.5), channel_id=1, replica_groups=mesh['dp'=32,'cent'=16] {'dp','cent'}, use_global_device_ids=true, to_apply=%region_11.12 | all-reduce | flops 1 | bytes 8 | tf_op jit(solution)/shard_map/psum | solution.py:74
  (10 shorter events, 0.1 us)
Async XLA Ops:
  7.2 135.5 %all-gather.4.cloned.1.call-start = ((), (), s32[]{:S(2)}) async-start(), calls=%async_computation | async-start | bytes 17825792 | tf_op jit(solution)/shard_map/all_gather | solution.py:30
  142.6 12.0 %copy-start.2 = (f32[256,1024]{1,0:T(8,128)S(1)}, f32[256,1024]{1,0:T(8,128)}, u32[]{:S(2)}) copy-start(f32[256,1024]{1,0:T(8,128)} %param.4) | copy-start | bytes 3145732
  161.3 2.7 copy-start
  242.2 4.6 %copy-start.1 = (f32[24,256,256]{1,2,0:T(8,128)S(1)}, f32[24,256,256]{1,2,0:T(8,128)}, u32[]{:S(2)}) copy-start(f32[24,256,256]{1,2,0:T(8,128)} %copy-done) | copy-start | bytes 18874372
Sparse Core Ops, SparseCore 0:
  11.0 131.6 all-gather.3
